TPU v7x, 32 devices: a whole 2x2x4 slice. The times are simulated.
32 devices in a mesh: fsdp: 4 (over y, x), rep: 8 (over z, core).
Axes of the slice: x: 2, y: 2, z: 4, core: 2. Of those that a mesh axis runs over, the one named last changes fastest.
Arguments:
- inputs: bfloat16 [8, 5120, 512], P('rep', 'fsdp'), may hold values from -6 to 6
- cotangent: bfloat16 [8, 5120, 512], P('rep', 'fsdp'), may hold values from -6 to 6
- segments: int32 [8, 5120], P('rep'), may hold values from 0 to 12, as said below
- trees: int32 [8, 5120], P('rep'), may hold values from 0 to 1, as said below
- parents: int32 [8, 2, 13], P('rep'), may hold values from 0 to 4, as said below
- w_query: bfloat16 [512, 512], P('fsdp'), may hold values from -0.25 to 0.25
- w_key: bfloat16 [512, 512], P('fsdp'), may hold values from -0.25 to 0.25
- w_value: bfloat16 [512, 512], P('fsdp'), may hold values from -0.25 to 0.25
- w_out: bfloat16 [512, 512], P('fsdp'), may hold values from -4 to 4
- w_hidden: bfloat16 [512, 2048], P('fsdp'), may hold values from -0.25 to 0.25
- w_proj: bfloat16 [2048, 512], P('fsdp'), may hold values from -0.125 to 0.125
- norm1_gain: float32 [512], replicated, may hold values from 0.1 to 1.9
- norm1_bias: float32 [512], replicated, may hold values from -3 to 3
- norm2_gain: float32 [512], replicated, may hold values from 0.1 to 1.9
- norm2_bias: float32 [512], replicated, may hold values from -3 to 3
Outputs:
- output: bfloat16 [8, 5120, 512], P('rep', 'fsdp')
- input_grad: float32 [8, 5120, 512], P('rep', 'fsdp')
- grad_query: float32 [512, 512], P('fsdp')
- grad_key: float32 [512, 512], P('fsdp')
- grad_value: float32 [512, 512], P('fsdp')
- grad_out: float32 [512, 512], P('fsdp')
- grad_hidden: float32 [512, 2048], P('fsdp')
- grad_proj: float32 [2048, 512], P('fsdp')
- grad_norm1_gain: float32 [512], replicated
- grad_norm1_bias: float32 [512], replicated
- grad_norm2_gain: float32 [512], replicated
- grad_norm2_bias: float32 [512], replicated
Inputs may be any that keep to these rules, and one draw needn't show every extreme that they name: Segment 0 of a tree is its trunk of 1024 tokens, segments 1 to 4 its branches and 5 to 12 its leaves, 128 tokens each; the tokens of a group come in aligned runs of 128 of one segment. `trees`: every tree has 2560 tokens in its group. `parents`: the trunk and the branches have parent 0; every leaf's parent is a branch, two leaves to a branch.
All inputs are finite; a program needn't handle non-finite values.
Results may differ from a plain program's by a relative error of at most 0.02.
Values may be sent and summed in bfloat16 or wider, within the bound.
A program may use at most 192 MiB of HBM per device.

v0:
```python
import jax
import jax.numpy as jnp
from jax import lax
from jax.sharding import PartitionSpec as P

HEADS = 8
KEY_BLOCK = 256


def norm_rows(h):
    centred = h - jnp.mean(h, axis=-1, keepdims=True)
    scale = lax.rsqrt(jnp.mean(centred * centred, axis=-1, keepdims=True) + 1e-05)
    return (centred * scale, scale)


def norm_back(grad_normed, normed, scale):
    return scale * (
        grad_normed
        - jnp.mean(grad_normed, axis=-1, keepdims=True)
        - normed * jnp.mean(grad_normed * normed, axis=-1, keepdims=True)
    )


def lookup(table, index):
    slots = jnp.arange(table.shape[0], dtype=jnp.int32)
    return jnp.sum(jnp.where(index[:, None] == slots[None, :], table[None, :], 0), axis=1)


def gelu_exact(values):
    return jax.nn.gelu(values, approximate=False)


def allowed_pair(seg_q, tree_q, first_q, second_q, pos_q, seg_k, tree_k, pos_k):
    same = seg_k[None, :] == seg_q[:, None]
    return (tree_k[None, :] == tree_q[:, None]) & (
        same & (pos_k[None, :] <= pos_q[:, None])
        | (seg_k[None, :] == first_q[:, None]) & (first_q != seg_q)[:, None]
        | (seg_k[None, :] == second_q[:, None]) & (second_q != first_q)[:, None]
    )


def shards(
    inputs,
    cotangent,
    segments,
    trees,
    parents,
    w_query,
    w_key,
    w_value,
    w_out,
    w_hidden,
    w_proj,
    norm1_gain,
    norm1_bias,
    norm2_gain,
    norm2_bias,
):
    single = jnp.float32
    half = jnp.bfloat16
    x = inputs[0]
    rows, width = x.shape
    heads = HEADS
    head_size = width // heads
    start = lax.axis_index("fsdp") * rows
    seg_all = segments[0]
    tree_all = trees[0]
    total = seg_all.shape[0]
    seg_count = parents.shape[2]
    table = parents[0].reshape(-1)
    first_all = lookup(table, tree_all * seg_count + seg_all)
    second_all = lookup(table, tree_all * seg_count + first_all)
    position = jnp.arange(total, dtype=jnp.int32)
    seg_q = lax.dynamic_slice_in_dim(seg_all, start, rows)
    tree_q = lax.dynamic_slice_in_dim(tree_all, start, rows)
    first_q = lax.dynamic_slice_in_dim(first_all, start, rows)
    second_q = lax.dynamic_slice_in_dim(second_all, start, rows)
    pos_q = lax.dynamic_slice_in_dim(position, start, rows)
    blocks = total // KEY_BLOCK

    def allowed_of(seg_k, tree_k, pos_k):
        return allowed_pair(seg_q, tree_q, first_q, second_q, pos_q, seg_k, tree_k, pos_k)

    weights = (
        lax.all_gather(w_query, "fsdp", axis=0, tiled=True),
        lax.all_gather(w_key, "fsdp", axis=0, tiled=True),
        lax.all_gather(w_value, "fsdp", axis=0, tiled=True),
        lax.all_gather(w_out, "fsdp", axis=0, tiled=True),
        lax.all_gather(w_hidden, "fsdp", axis=0, tiled=True),
        lax.all_gather(w_proj, "fsdp", axis=0, tiled=True),
    )
    full_q, full_k, full_v, full_o, full_h, full_p = weights
    query = jnp.dot(x, full_q, preferred_element_type=single).astype(half)
    own_keys = jnp.dot(x, full_k, preferred_element_type=single).astype(half)
    own_values = jnp.dot(x, full_v, preferred_element_type=single).astype(half)
    keys_all, values_all = (
        lax.all_gather(own_keys, "fsdp", axis=0, tiled=True),
        lax.all_gather(own_values, "fsdp", axis=0, tiled=True),
    )
    q_heads = query.reshape(rows, heads, head_size)
    items = (
        keys_all.reshape(blocks, KEY_BLOCK, heads, head_size),
        values_all.reshape(blocks, KEY_BLOCK, heads, head_size),
        seg_all.reshape(blocks, KEY_BLOCK),
        tree_all.reshape(blocks, KEY_BLOCK),
        position.reshape(blocks, KEY_BLOCK),
    )

    def scores_of(item):
        raw = jnp.einsum("rhd,khd->hrk", q_heads, item[0], preferred_element_type=single) * 0.125
        return jnp.where(allowed_of(item[2], item[3], item[4])[None], raw, -jnp.inf)

    def stats_step(carry, item):
        top, mass = carry
        scores = scores_of(item)
        new_top = jnp.maximum(top, jnp.max(scores, axis=-1))
        mass = mass * jnp.exp(top - new_top) + jnp.sum(
            jnp.exp(scores - new_top[..., None]), axis=-1
        )
        return ((new_top, mass), None)

    start_stats = (jnp.full((heads, rows), -1e30, single), jnp.zeros((heads, rows), single))
    (top, mass), _ = lax.scan(stats_step, start_stats, items)
    log_total = top + jnp.log(mass)

    def probs_of(item):
        return jnp.exp(scores_of(item) - log_total[..., None])

    def context_step(acc, item):
        probs = probs_of(item).astype(half)
        return (
            acc + jnp.einsum("hrk,khd->rhd", probs, item[1], preferred_element_type=single),
            None,
        )

    acc, _ = lax.scan(context_step, jnp.zeros((rows, heads, head_size), single), items)
    context = acc.reshape(rows, width).astype(half)
    attended = jnp.dot(context, full_o, preferred_element_type=single)
    normed1, scale1 = norm_rows(x.astype(single) + attended)
    mid = normed1 * norm1_gain + norm1_bias
    mid_low = mid.astype(half)
    pre = jnp.dot(mid_low, full_h, preferred_element_type=single)
    act, act_back = jax.vjp(gelu_exact, pre)
    act_low = act.astype(half)
    normed2, scale2 = norm_rows(mid + jnp.dot(act_low, full_p, preferred_element_type=single))
    output = (normed2 * norm2_gain + norm2_bias).astype(half)
    weights = (
        lax.all_gather(w_query, "fsdp", axis=0, tiled=True),
        lax.all_gather(w_key, "fsdp", axis=0, tiled=True),
        lax.all_gather(w_value, "fsdp", axis=0, tiled=True),
        lax.all_gather(w_out, "fsdp", axis=0, tiled=True),
        lax.all_gather(w_hidden, "fsdp", axis=0, tiled=True),
        lax.all_gather(w_proj, "fsdp", axis=0, tiled=True),
    )
    full_q, full_k, full_v, full_o, full_h, full_p = weights
    grad_rows = cotangent[0].astype(single)
    gain2 = jnp.sum(grad_rows * normed2, axis=0)
    bias2 = jnp.sum(grad_rows, axis=0)
    grad_second = norm_back(grad_rows * norm2_gain, normed2, scale2)
    grad_branch = grad_second.astype(half)
    proj_grad = jnp.einsum("rf,rd->fd", act_low, grad_branch, preferred_element_type=single)
    grad_act = jnp.einsum("rd,fd->rf", grad_branch, full_p, preferred_element_type=single)
    grad_pre = act_back(grad_act)[0].astype(half)
    hidden_grad = jnp.einsum("rd,rf->df", mid_low, grad_pre, preferred_element_type=single)
    grad_mid = grad_second + jnp.einsum(
        "rf,df->rd", grad_pre, full_h, preferred_element_type=single
    )
    gain1 = jnp.sum(grad_mid * normed1, axis=0)
    bias1 = jnp.sum(grad_mid, axis=0)
    grad_first = norm_back(grad_mid * norm1_gain, normed1, scale1)
    grad_att = grad_first.astype(half)
    out_grad = jnp.einsum("rd,re->de", context, grad_att, preferred_element_type=single)
    grad_context = jnp.einsum("re,de->rd", grad_att, full_o, preferred_element_type=single).astype(
        half
    )
    grad_heads = grad_context.reshape(rows, heads, head_size)

    def delta_step(delta, item):
        probs = probs_of(item)
        grad_probs = jnp.einsum("rhd,khd->hrk", grad_heads, item[1], preferred_element_type=single)
        return (delta + jnp.sum(probs * grad_probs, axis=-1), None)

    delta, _ = lax.scan(delta_step, jnp.zeros((heads, rows), single), items)

    def back_step(grad_query, item):
        probs = probs_of(item)
        grad_probs = jnp.einsum("rhd,khd->hrk", grad_heads, item[1], preferred_element_type=single)
        grad_scores = (probs * (grad_probs - delta[..., None])).astype(half)
        grad_query = (
            grad_query
            + jnp.einsum("hrk,khd->rhd", grad_scores, item[0], preferred_element_type=single)
            * 0.125
        )
        key_part = (
            jnp.einsum("hrk,rhd->khd", grad_scores, q_heads, preferred_element_type=single) * 0.125
        )
        value_part = jnp.einsum(
            "hrk,rhd->khd", probs.astype(half), grad_heads, preferred_element_type=single
        )
        return (grad_query, (key_part, value_part))

    grad_query, parts = lax.scan(back_step, jnp.zeros((rows, heads, head_size), single), items)
    key_terms = parts[0].reshape(total, width)
    value_terms = parts[1].reshape(total, width)
    key_grad, value_grad = (
        lax.psum_scatter(
            key_terms.astype(jnp.bfloat16), "fsdp", scatter_dimension=0, tiled=True
        ).astype(jnp.float32),
        lax.psum_scatter(
            value_terms.astype(jnp.bfloat16), "fsdp", scatter_dimension=0, tiled=True
        ).astype(jnp.float32),
    )
    key_low = key_grad.astype(half)
    value_low = value_grad.astype(half)
    query_low = grad_query.reshape(rows, width).astype(half)
    input_grad = (
        grad_first
        + jnp.einsum("re,de->rd", query_low, full_q, preferred_element_type=single)
        + jnp.einsum("re,de->rd", key_low, full_k, preferred_element_type=single)
        + jnp.einsum("re,de->rd", value_low, full_v, preferred_element_type=single)
    )
    query_w = jnp.einsum("rd,re->de", x, query_low, preferred_element_type=single)
    key_w = jnp.einsum("rd,re->de", x, key_low, preferred_element_type=single)
    value_w = jnp.einsum("rd,re->de", x, value_low, preferred_element_type=single)
    shares = (
        lax.psum_scatter(
            query_w.astype(jnp.bfloat16), "fsdp", scatter_dimension=0, tiled=True
        ).astype(jnp.float32),
        lax.psum_scatter(
            key_w.astype(jnp.bfloat16), "fsdp", scatter_dimension=0, tiled=True
        ).astype(jnp.float32),
        lax.psum_scatter(
            value_w.astype(jnp.bfloat16), "fsdp", scatter_dimension=0, tiled=True
        ).astype(jnp.float32),
        lax.psum_scatter(
            out_grad.astype(jnp.bfloat16), "fsdp", scatter_dimension=0, tiled=True
        ).astype(jnp.float32),
        lax.psum_scatter(
            hidden_grad.astype(jnp.bfloat16), "fsdp", scatter_dimension=0, tiled=True
        ).astype(jnp.float32),
        lax.psum_scatter(
            proj_grad.astype(jnp.bfloat16), "fsdp", scatter_dimension=0, tiled=True
        ).astype(jnp.float32),
    )
    shares = (
        lax.psum(shares[0].astype(jnp.bfloat16), "rep").astype(jnp.float32),
        lax.psum(shares[1].astype(jnp.bfloat16), "rep").astype(jnp.float32),
        lax.psum(shares[2].astype(jnp.bfloat16), "rep").astype(jnp.float32),
        lax.psum(shares[3].astype(jnp.bfloat16), "rep").astype(jnp.float32),
        lax.psum(shares[4].astype(jnp.bfloat16), "rep").astype(jnp.float32),
        lax.psum(shares[5].astype(jnp.bfloat16), "rep").astype(jnp.float32),
    )
    norms = lax.psum((gain1, bias1, gain2, bias2), ("fsdp", "rep"))
    return (
        output[None],
        input_grad[None],
        shares[0],
        shares[1],
        shares[2],
        shares[3],
        shares[4],
        shares[5],
        norms[0],
        norms[1],
        norms[2],
        norms[3],
    )


def solution(mesh):
    placed = (
        P("rep", "fsdp", None),
        P("rep", "fsdp", None),
        P("rep", None),
        P("rep", None),
        P("rep", None, None),
        P("fsdp", None),
        P("fsdp", None),
        P("fsdp", None),
        P("fsdp", None),
        P("fsdp", None),
        P("fsdp", None),
        P(),
        P(),
        P(),
        P(),
    )
    return jax.shard_map(
        shards,
        mesh=mesh,
        in_specs=placed,
        out_specs=(
            P("rep", "fsdp", None),
            P("rep", "fsdp", None),
            P("fsdp", None),
            P("fsdp", None),
            P("fsdp", None),
            P("fsdp", None),
            P("fsdp", None),
            P("fsdp", None),
            P(),
            P(),
            P(),
            P(),
        ),
        check_vma=False,
    )
```

profile of v0, /device:TPU:0, one launch (start us, length us, event | category | flops | bytes accessed | tf_op | source)
XLA Modules:
  0.0 2056.1 jit_solution(4566805571781801535)
XLA Ops:
  7.2 11.8 all_gather.32
  22.6 10.4 all_gather.30
  43.0 11.4 all_gather.34
  57.5 15.0 all_gather.35
  74.9 16.3 all-gather.7.cloned.1.call-done
  91.2 14.0 reshape.917
  105.2 11.1 copy.109
  116.3 411.2 %while.54 = (s32[]{:T(128)}, f32[8,1280]{1,0:T(8,128)S(1)}, f32[8,1280]{1,0:T(8,128)}, s32[20,256]{1,0:T(8,128)}, s32[1280]{0:T(1024)S(1)}, /*index=5*/s32[20,25...) while((s32[]{:T(128)}, f32[8,1280]{1,0:T(8,128)S(1)}, ...), condition=%wide.region_5.6_spmd.clone, body=%wide.region_2.5_spmd.clone.sunk | while | flops 357550080 | bytes 24635912 | solution.py:123
  527.5 13.9 reshape.916
  541.4 11.1 copy.108
  553.1 227.5 %while.55 = (s32[]{:T(128)}, f32[1280,8,64]{0,2,1:T(8,128)}, bf16[20,256,8,64]{1,3,2,0:T(8,128)(2,1)}, s32[20,256]{1,0:T(8,128)}, s32[1280]{0:T(1024)S(1)}, /*in...) while((s32[]{:T(128)}, f32[1280,8,64]{0,2,1:T(8,128)}, ...), condition=%wide.region_7.8_spmd.clone, body=%wide.region_6.7_spmd.clone.sunk | while | flops 686489600 | bytes 7817921 | solution.py:136
  785.4 29.8 %multiply_convert_fusion = (bf16[1280,2048]{1,0:T(8,128)(2,1)}, f32[1280,2048]{1,0:T(8,128)}, f32[1280,2048]{1,0:T(8,128)}) fusion(bf16[512,2048]{1,0:T(8,128)(2,1)} %all-gather.9.cloned.1.call-done, f32[1280,512]{0,1:T(8,128)} %copy-done.3, f32[512]{0:T(512)S(1)} %copy-done.69, f32[512]{0:T(512)S(1)} %copy-done.64, f32[1280]{0:T(1024)S(1)} %add_rsqrt_fusion.1, ...), kind=kOutput, calls=%fused_computation.83 | convolution fusion | flops 2858024960 | bytes 30947328 | tf_op jit(solution)/shard_map/dot_general | solution.py:142
  827.6 12.7 add_convert_fusion
  851.0 235.5 %while.56 = (s32[]{:T(128)}, f32[8,1280]{1,0:T(8,128)S(1)}, s32[20,256]{1,0:T(8,128)}, s32[1280]{0:T(1024)S(1)}, s32[20,256]{1,0:T(8,128)}, /*index=5*/s32[1280]...) while((s32[]{:T(128)}, f32[8,1280]{1,0:T(8,128)S(1)}, ...), condition=%wide.region_18.19_spmd.clone, body=%wide.region_16.18_spmd.clone.sunk | while | flops 687810560 | bytes 25021128 | solution.py:183
  1086.5 565.8 %while.57 = (s32[]{:T(128)}, f32[1280,8,64]{0,2,1:T(8,128)}, bf16[20,256,8,64]{1,3,2,0:T(8,128)(2,1)}, bf16[20,256,8,64]{1,3,2,0:T(8,128)(2,1)}, bf16[20,256,8,6...) while((s32[]{:T(128)}, f32[1280,8,64]{0,2,1:T(8,128)}, ...), condition=%wide.region_20.21_spmd.clone, body=%wide.region_19.20_spmd.clone.sunk | while | flops 1709637632 | bytes 165515600 | solution.py:202
  1676.8 47.0 %reduce-scatter.15.cloned.1.call-done = bf16[1280,512]{0,1:T(8,128)(2,1)} async-done(((bf16[5120,512]{0,1:T(8,128)(2,1)}), bf16[1280,512]{0,1:T(8,128)(2,1)}) %reduce-scatter.15.cloned.1.call-update) | async-done | bytes 1310736 | tf_op jit(solution)/shard_map/reduce_scatter | solution.py:206
  1727.0 61.0 %reduce-scatter.17.cloned.1.call-done = bf16[1280,512]{0,1:T(8,128)(2,1)} async-done(((bf16[5120,512]{0,1:T(8,128)(2,1)}), bf16[1280,512]{0,1:T(8,128)(2,1)}) %reduce-scatter.17.cloned.1.call-update) | async-done | bytes 1310736 | tf_op jit(solution)/shard_map/reduce_scatter | solution.py:209
  1817.4 26.2 %reduce-scatter.27.cloned.1.call-done = bf16[128,512]{1,0:T(8,128)(2,1)} async-done(((bf16[512,512]{1,0:T(8,128)(2,1)}), bf16[128,512]{1,0:T(8,128)(2,1)}) %reduce-scatter.27.cloned.1.call-update) | async-done | bytes 131088
  1845.2 26.0 %reduce-scatter.29.cloned.1.call-done = bf16[128,512]{1,0:T(8,128)(2,1)} async-done(((bf16[512,512]{1,0:T(8,128)(2,1)}), bf16[128,512]{1,0:T(8,128)(2,1)}) %reduce-scatter.29.cloned.1.call-update) | async-done | bytes 131088
  1872.9 26.0 %reduce-scatter.19.cloned.1.call-done = bf16[128,512]{1,0:T(8,128)(2,1)} async-done(((bf16[512,512]{1,0:T(8,128)(2,1)}), bf16[128,512]{1,0:T(8,128)(2,1)}) %reduce-scatter.19.cloned.1.call-update) | async-done | bytes 131088 | tf_op jit(solution)/shard_map/reduce_scatter | solution.py:235
  1898.9 38.2 %reduce-scatter.23.cloned.1.call-done = bf16[512,512]{1,0:T(8,128)(2,1)} async-done(((bf16[2048,512]{1,0:T(8,128)(2,1)}), bf16[512,512]{1,0:T(8,128)(2,1)}) %reduce-scatter.23.cloned.1.call-update) | async-done | bytes 524304 | tf_op jit(solution)/shard_map/reduce_scatter | solution.py:241
  1937.1 38.3 %reduce-scatter.21.cloned.1.call-done = bf16[128,2048]{1,0:T(8,128)(2,1)} async-done(((bf16[512,2048]{1,0:T(8,128)(2,1)}), bf16[128,2048]{1,0:T(8,128)(2,1)}) %reduce-scatter.21.cloned.1.call-update) | async-done | bytes 524304 | tf_op jit(solution)/shard_map/reduce_scatter | solution.py:238
  1981.1 40.0 %all-reduce = (f32[512]{0:T(512)}, f32[512]{0:T(512)}, f32[512]{0:T(512)}, f32[512]{0:T(512)}) all-reduce(f32[512]{0:T(512)S(1)} %copy-done.66, f32[512]{0:T(512)S(1)} %copy-done.67, f32[512]{0:T(512)S(1)} %copy-done.56, f32[512]{0:T(512)S(1)} %convert_reduce_fusion), channel_id=1, replica_groups=mesh['fsdp'=4,'rep'=8] {'fsdp','rep'}, use_global_device_ids=true, to_apply=%region_36.37 | all-reduce | flops 2048 | bytes 16384 | tf_op jit(solution)/shard_map/psum | solution.py:253
  2029.5 12.0 all-reduce.4.cloned.1.call-done
  (1500 shorter events, 1561.9 us)
Async XLA Ops:
  7.2 84.0 %all-gather.7.cloned.1.call-start = ((), (), s32[]{:S(2)}) async-start(), calls=%async_computation.9 | async-start | bytes 6553600 | tf_op jit(solution)/shard_map/all_gather | solution.py:97
  22.5 505.0 %all-gather.5.cloned.1.call-start = ((), (), s32[]{:S(2)}) async-start(), calls=%async_computation.8 | async-start | bytes 6553600 | tf_op jit(solution)/shard_map/all_gather | solution.py:98
  35.0 750.4 %all-gather.9.cloned.1.call-start = ((), (), s32[]{:S(2)}) async-start(), calls=%async_computation.10 | async-start | bytes 2621440 | tf_op jit(solution)/shard_map/all_gather | solution.py:89
  35.7 779.6 %all-gather.11.cloned.1.call-start = ((), (), s32[]{:S(2)}) async-start(), calls=%async_computation.11 | async-start | bytes 2621440 | tf_op jit(solution)/shard_map/all_gather | solution.py:90
  36.3 1687.5 %reduce-scatter.15.cloned.1.call-start = ((), (), s32[]{:S(2)}) async-start(), calls=%async_computation.12 | async-start | bytes 6553600 | tf_op jit(solution)/shard_map/reduce_scatter | solution.py:206
  40.6 16.9 copy-start.41
  783.6 64.4 %copy-start.49 = (f32[1280]{0:T(1024)}, f32[1280]{0:T(1024)S(1)}, u32[]{:S(2)}) copy-start(f32[1280]{0:T(1024)S(1)} %broadcast_multiply_fusion.6) | copy-start | bytes 15364
  785.4 62.6 %copy-start.53 = (f32[1280]{0:T(1024)}, f32[1280]{0:T(1024)S(1)}, u32[]{:S(2)}) copy-start(f32[1280]{0:T(1024)S(1)} %add_rsqrt_fusion.1) | copy-start | bytes 15364
  822.4 17.8 copy-start.8
  822.5 17.8 copy-start.47
  1662.2 125.9 %reduce-scatter.17.cloned.1.call-start = ((), (), s32[]{:S(2)}) async-start(), calls=%async_computation.13 | async-start | bytes 6553600 | tf_op jit(solution)/shard_map/reduce_scatter | solution.py:209
  1672.3 143.4 %reduce-scatter.25.cloned.1.call-start = ((), (), s32[]{:S(2)}) async-start(), calls=%async_computation.17 | async-start | bytes 655360
  1676.4 111.6 %copy-start.37 = (bf16[1,1280,512]{2,1,0:T(8,128)(2,1)S(1)}, bf16[1,1280,512]{2,1,0:T(8,128)(2,1)}, u32[]{:S(2)}) copy-start(bf16[1,1280,512]{2,1,0:T(8,128)(2,1)} %param.23) | copy-start | bytes 3932164
  1676.5 167.1 %reduce-scatter.27.cloned.1.call-start = ((), (), s32[]{:S(2)}) async-start(), calls=%async_computation.18 | async-start | bytes 655360
  1727.0 64.4 %copy-start.10 = (bf16[1280,8,64]{0,2,1:T(8,128)(2,1)S(1)}, bf16[1280,8,64]{0,2,1:T(8,128)(2,1)}, u32[]{:S(2)}) copy-start(bf16[1280,8,64]{0,2,1:T(8,128)(2,1)} %copy-done.9) | copy-start | bytes 3932164
  1727.0 144.2 %reduce-scatter.29.cloned.1.call-start = ((), (), s32[]{:S(2)}) async-start(), calls=%async_computation.19 | async-start | bytes 655360
  1791.3 107.6 %reduce-scatter.19.cloned.1.call-start = ((), (), s32[]{:S(2)}) async-start(), calls=%async_computation.14 | async-start | bytes 655360 | tf_op jit(solution)/shard_map/reduce_scatter | solution.py:235
  1795.0 142.1 %reduce-scatter.23.cloned.1.call-start = ((), (), s32[]{:S(2)}) async-start(), calls=%async_computation.16 | async-start | bytes 2621440 | tf_op jit(solution)/shard_map/reduce_scatter | solution.py:241
  1803.1 172.3 %reduce-scatter.21.cloned.1.call-start = ((), (), s32[]{:S(2)}) async-start(), calls=%async_computation.15 | async-start | bytes 2621440 | tf_op jit(solution)/shard_map/reduce_scatter | solution.py:238
  1810.9 164.5 %copy-start.12 = (bf16[1280,8,64]{0,2,1:T(8,128)(2,1)S(1)}, bf16[1280,8,64]{0,2,1:T(8,128)(2,1)}, u32[]{:S(2)}) copy-start(bf16[1280,8,64]{0,2,1:T(8,128)(2,1)} %copy-done.11) | copy-start | bytes 3932164
  1810.9 164.5 %copy-start.29 = (bf16[512,512]{1,0:T(8,128)(2,1)S(1)}, bf16[512,512]{1,0:T(8,128)(2,1)}, u32[]{:S(2)}) copy-start(bf16[512,512]{1,0:T(8,128)(2,1)} %copy-done.28) | copy-start | bytes 1572868
  1811.0 230.5 %all-reduce.4.cloned.1.call-start = ((), (), s32[]{:S(2)}) async-start(), calls=%async_computation.20 | async-start | bytes 3145728 | tf_op jit(solution)/shard_map/psum | solution.py:246
  1979.6 41.5 %copy-start.25 = (bf16[512,512]{1,0:T(8,128)(2,1)S(1)}, bf16[512,512]{1,0:T(8,128)(2,1)}, u32[]{:S(2)}) copy-start(bf16[512,512]{1,0:T(8,128)(2,1)} %copy-done.24) | copy-start | bytes 1572868
  1979.6 41.5 %copy-start.33 = (bf16[1280,512]{0,1:T(8,128)(2,1)S(1)}, bf16[1280,512]{0,1:T(8,128)(2,1)}, u32[]{:S(2)}) copy-start(bf16[1280,512]{0,1:T(8,128)(2,1)} %reduce-scatter.15.cloned.1.call-done) | copy-start | bytes 3932164
  (346 other events, 2033.7 us)
Sparse Core Ops, SparseCore 0:
  22.7 68.5 all-gather.6
  93.1 61.4 all-gather.4
  156.4 35.3 all-gather.8
  193.4 35.2 all-gather.10
  1662.3 61.4 reduce-scatter.14
  1726.6 61.4 reduce-scatter.16
  1790.9 24.7 reduce-scatter.24
  1818.7 24.7 reduce-scatter.26
  1846.4 24.7 reduce-scatter.28
  1874.1 24.7 reduce-scatter.18
  1901.9 35.1 reduce-scatter.22
  1940.2 35.1 reduce-scatter.20
  1978.8 62.6 all-reduce.3
where the time goes:
time: 2080 us; the launch traced here: 2060 us
  matrix products  920 us (44%)
  other arithmetic  407 us (20%)
  local copies, waits for them, and re-layouts  321 us (15%)
  waiting for transfers between devices  297 us (14%)
  blocking collectives  88.7 us (4%)
    dot_general x60, matrix products, scores_of(): jnp.einsum('rhd,khd->hrk', q_heads, item[0], preferred_element_type=single)  279 us
    dot_general x20, matrix products, context_step(): jnp.einsum('hrk,khd->rhd', probs, item[1], preferred_element_type=single)  138 us
    dynamic_slice x160, local copies, waits for them, and re-layouts, shards(): (top, mass), _ = lax.scan(stats_step, start_stats, items)  137 us
    and x80, other arithmetic, allowed_pair(): (tree_k[None, :] == tree_q[:, None]) & (same & (pos_k[None, :] <= pos_q[:...  128 us
    reduce_sum x20, other arithmetic, stats_step(): jnp.sum(jnp.exp(scores - new_top[..., None]), axis=-1)  124 us
    dot_general x20, matrix products, back_step(): jnp.einsum('hrk,khd->rhd', grad_scores, item[0], preferred_element_type=s...  120 us
    dot_general x20, matrix products, back_step(): jnp.einsum('rhd,khd->hrk', grad_heads, item[1], preferred_element_type=si...  95.3 us
    dot_general x20, matrix products, back_step(): jnp.einsum('hrk,rhd->khd', probs.astype(half), grad_heads, preferred_elem...  89.4 us
  transfers between devices with their start and end apart: 13, of which 10 were waited for; matrix products, arithmetic and copies ran while one was open for 38% of the time, Pallas kernels for 0%

commit v1 on v0

v1 whole, which is shorter than its diff:
```python
import functools

import jax
import jax.numpy as jnp
from jax import lax
from jax.experimental import pallas as pl
from jax.experimental.pallas import tpu as pltpu
from jax.sharding import PartitionSpec as P

HEADS = 8
HEAD = 64
BLOCK = 128
PAIR = 2 * BLOCK
TRUNK = 8
BRANCHES = 4
LEAVES = 8
TREE_BLOCKS = TRUNK + BRANCHES + LEAVES
TREE_TOK = TREE_BLOCKS * BLOCK
SINGLE = jnp.float32
HALF = jnp.bfloat16
NN = (((1,), (0,)), ((), ()))
NT = (((1,), (1,)), ((), ()))
LOG2E = 1.4426950408889634
SCALE = 0.125 * LOG2E
VMEM_LIMIT = 58 << 20


def dot(left, right, dims=NN):
    return lax.dot_general(left, right, dims, preferred_element_type=SINGLE)


def row_mean(values):
    return jnp.mean(values, axis=-1, keepdims=True)


def block_order(segments, trees, parents, rows, me):
    seg = segments.reshape(-1, BLOCK)[:, 0]
    tree = trees.reshape(-1, BLOCK)[:, 0]
    count = seg.shape[0]
    table = parents.reshape(-1)
    slot = tree * parents.shape[1] + seg
    parent = jnp.sum(
        jnp.where(slot[:, None] == jnp.arange(table.shape[0])[None, :], table[None, :], 0), axis=1
    )
    place = jnp.arange(count, dtype=jnp.int32)
    kind = jnp.where(seg == 0, 0, jnp.where(seg <= BRANCHES, seg, 16 * parent + seg))
    key = (tree * 256 + kind) * 64 + place
    rank = jnp.sum((key[None, :] < key[:, None]).astype(jnp.int32), axis=1)
    per = rows // BLOCK
    near = ((place // per) ^ me) * per + place % per
    order = jnp.sum(jnp.where(rank[None, :] == place[:, None], near[None, :], 0), axis=1)
    return order.astype(jnp.int32)


def tile_list():
    out = []
    trunk = TRUNK * BLOCK
    for start in range(0, trunk, PAIR):
        keys = [(0, start, None)] if start else []
        out.append((start, keys + [(start, PAIR, "causal")]))
    for pair in range(BRANCHES // 2):
        start = trunk + pair * PAIR
        out.append((start, [(0, trunk, None), (start, PAIR, "own")]))
    for branch in range(BRANCHES):
        start = trunk + BRANCHES * BLOCK + branch * PAIR
        out.append(
            (
                start,
                [(0, trunk, None), (trunk + branch * BLOCK, BLOCK, None), (start, PAIR, "own")],
            )
        )
    return out


def mask_of(kind):
    key = lax.broadcasted_iota(jnp.int32, (PAIR, PAIR), 0)
    query = lax.broadcasted_iota(jnp.int32, (PAIR, PAIR), 1)
    mask = key <= query
    if kind == "own":
        mask = mask & ((key >= BLOCK) == (query >= BLOCK))
    return mask


def pair_rows(order_ref, tree, start):
    first = tree * TREE_BLOCKS + start // BLOCK
    return [pl.ds(pl.multiple_of(order_ref[first + i] * BLOCK, BLOCK), BLOCK) for i in range(2)]


def attend_kernel(
    heads, order_ref, x_ref, w_ref, ctx_ref, q_ref, k_ref, v_ref, kt_ref, ot_ref, lse_ref, vt_ref
):
    trees = q_ref.shape[0] // heads
    wide = heads * HEAD

    def project(step, _):
        tree = step // (TREE_BLOCKS // 2)
        start = pl.multiple_of((step % (TREE_BLOCKS // 2)) * PAIR, PAIR)
        rows = [
            pl.ds(pl.multiple_of(order_ref[2 * step + i] * BLOCK, BLOCK), BLOCK) for i in range(2)
        ]
        x = jnp.concatenate([x_ref[r, :] for r in rows], axis=0)
        out = dot(x, w_ref[...]).astype(HALF)
        here = pl.ds(start, PAIR)
        kt = out[:, wide : 2 * wide].T
        vt = out[:, 2 * wide :].T
        for h in range(heads):
            at = tree * heads + h
            cols = slice(h * HEAD, (h + 1) * HEAD)
            q_ref[at, here, :] = out[:, cols]
            k_ref[at, here, :] = out[:, wide:][:, cols]
            v_ref[at, here, :] = out[:, 2 * wide :][:, cols]
            kt_ref[at, :, here] = kt[cols]
            vt_ref[at, :, here] = vt[cols]
        return 0

    lax.fori_loop(0, trees * TREE_BLOCKS // 2, project, 0)

    def tree_step(tree, _):
        for start, keys in tile_list():
            outs = []
            for h in range(heads):
                at = tree * heads + h
                q = q_ref[at, start : start + PAIR, :]
                scores = []
                for off, size, kind in keys:
                    s = dot(k_ref[at, off : off + size, :], q, NT)
                    if kind:
                        s = jnp.where(mask_of(kind), s, -1e30)
                    scores.append(s)
                top = functools.reduce(
                    jnp.maximum, [jnp.max(s, axis=0, keepdims=True) for s in scores]
                )
                top = top * SCALE
                mass = 0.0
                acc = 0.0
                for (off, size, _), s in zip(keys, scores):
                    e = jnp.exp2(s * SCALE - top)
                    mass = mass + jnp.sum(e, axis=0, keepdims=True)
                    acc = acc + dot(vt_ref[at, :, off : off + size], e.astype(HALF))
                outs.append(acc * (1.0 / mass))
                lse_ref[at, :, start : start + PAIR] = top + jnp.log2(mass)
            out = jnp.concatenate(outs, axis=0) if heads > 1 else outs[0]
            ot_ref[tree, :, start : start + PAIR] = out
            ctx = out.T.astype(HALF)
            for i, r in enumerate(pair_rows(order_ref, tree, start)):
                ctx_ref[r, :] = ctx[i * BLOCK : (i + 1) * BLOCK]
        return 0

    lax.fori_loop(0, trees, tree_step, 0)


def vmem(count):
    return [pl.BlockSpec(memory_space=pltpu.VMEM)] * count


def shape(dims, dtype):
    return jax.ShapeDtypeStruct(dims, dtype)


def attend(order, x, w, heads):
    total = x.shape[0]
    trees = total // TREE_TOK
    n = trees * heads
    return pl.pallas_call(
        functools.partial(attend_kernel, heads),
        out_shape=[
            shape((total, heads * HEAD), HALF),
            shape((n, TREE_TOK, HEAD), HALF),
            shape((n, TREE_TOK, HEAD), HALF),
            shape((n, TREE_TOK, HEAD), HALF),
            shape((n, HEAD, TREE_TOK), HALF),
            shape((trees, heads * HEAD, TREE_TOK), SINGLE),
            shape((n, 1, TREE_TOK), SINGLE),
        ],
        in_specs=[pl.BlockSpec(memory_space=pltpu.SMEM)] + vmem(2),
        out_specs=vmem(7),
        scratch_shapes=[pltpu.VMEM((n, HEAD, TREE_TOK), HALF)],
        compiler_params=pltpu.CompilerParams(vmem_limit_bytes=VMEM_LIMIT),
        cost_estimate=pl.CostEstimate(
            flops=10 * 10**9, bytes_accessed=20 * 10**6, transcendentals=11 * 10**6
        ),
        name="attend",
    )(order, x, w)


def pack_grads(me, parts, ao, ah, ap, pack_ref):
    width = ao.shape[1]
    depth = ao.shape[0] // parts
    inner = ah.shape[1]
    cols = inner // parts
    for c in range(parts):
        to = c ^ me
        pack_ref[to, 0:depth, :] = ao[c * depth : (c + 1) * depth, :].astype(HALF)
        for j in range(inner // width):
            pack_ref[to, depth * (j + 1) : depth * (j + 2), :] = ah[
                c * depth : (c + 1) * depth, j * width : (j + 1) * width
            ].astype(HALF)
        base = depth * (1 + inner // width)
        piece = ap[:, c * cols : (c + 1) * cols].astype(HALF)
        for j in range(width // cols):
            pack_ref[to, base : base + cols, j * cols : (j + 1) * cols] = piece[
                j * cols : (j + 1) * cols
            ]


def forward_back_kernel(
    chunk,
    me_ref,
    x_ref,
    ctx_ref,
    dy_ref,
    wo_ref,
    wh_ref,
    wp_ref,
    vec_ref,
    out_ref,
    dh1_ref,
    dctx_ref,
    pack_ref,
    norm_ref,
    ao,
    ah,
    ap,
    g_s,
    d_s,
):
    step = pl.program_id(0)
    me = me_ref[0]
    parts = ctx_ref.shape[0]
    inner = wh_ref.shape[1]
    gain1, bias1 = vec_ref[0:1, :], vec_ref[1:2, :]
    gain2, bias2 = vec_ref[2:3, :], vec_ref[3:4, :]

    @pl.when(step == 0)
    def _():
        for ref in (ao, ah, ap, norm_ref):
            ref[...] = jnp.zeros_like(ref)

    ctx = jnp.concatenate([ctx_ref[c ^ me] for c in range(parts)], axis=-1)
    h1 = x_ref[...].astype(SINGLE) + dot(ctx, wo_ref[...])
    c1 = h1 - row_mean(h1)
    r1 = lax.rsqrt(row_mean(c1 * c1) + 1e-5)
    n1 = c1 * r1
    y1 = n1 * gain1 + bias1
    u = y1.astype(HALF)
    branch = 0.0
    for j in range(0, inner, chunk):
        s = slice(j, j + chunk)
        z = dot(u, wh_ref[:, s])
        cdf = 0.5 * (1.0 + lax.erf(z * 0.7071067811865476))
        pdf = jnp.exp2(z * z * (-0.5 * LOG2E)) * 0.3989422804014327
        g = (z * cdf).astype(HALF)
        g_s[:, s] = g
        d_s[:, s] = cdf + z * pdf
        branch = branch + dot(g, wp_ref[s, :])
    h2 = y1 + branch
    c2 = h2 - row_mean(h2)
    r2 = lax.rsqrt(row_mean(c2 * c2) + 1e-5)
    n2 = c2 * r2
    out_ref[...] = (n2 * gain2 + bias2).astype(HALF)
    dy = dy_ref[...].astype(SINGLE)
    norm_ref[2:3, :] += jnp.sum(dy * n2, axis=0, keepdims=True)
    norm_ref[3:4, :] += jnp.sum(dy, axis=0, keepdims=True)
    dn2 = dy * gain2
    dh2 = r2 * (dn2 - row_mean(dn2) - n2 * row_mean(dn2 * n2))
    df = dh2.astype(HALF)
    df_t = df.T
    u_t = u.T
    back = 0.0
    for j in range(0, inner, chunk):
        s = slice(j, j + chunk)
        dz = (dot(df, wp_ref[s, :], NT) * d_s[:, s]).astype(HALF)
        back = back + dot(dz, wh_ref[:, s], NT)
        ap[:, s] += dot(df_t, g_s[:, s])
        ah[:, s] += dot(u_t, dz)
    dy1 = dh2 + back
    norm_ref[0:1, :] += jnp.sum(dy1 * n1, axis=0, keepdims=True)
    norm_ref[1:2, :] += jnp.sum(dy1, axis=0, keepdims=True)
    dn1 = dy1 * gain1
    dh1 = r1 * (dn1 - row_mean(dn1) - n1 * row_mean(dn1 * n1))
    dh1_ref[...] = dh1
    da = dh1.astype(HALF)
    ao[...] += dot(ctx.T, da)
    dctx = dot(da, wo_ref[...], NT).astype(HALF)
    wide = dctx.shape[1] // parts
    for c in range(parts):
        dctx_ref[c ^ me] = dctx[:, c * wide : (c + 1) * wide]

    @pl.when(step == pl.num_programs(0) - 1)
    def _():
        pack_grads(me, parts, ao, ah, ap, pack_ref)


def forward_back(me, x, ctx, dy, wo, wh, wp, vec):
    rows, width = x.shape
    parts, _, wide = ctx.shape
    inner = wh.shape[1]
    tile = PAIR if rows % PAIR == 0 else BLOCK
    packed = (width // parts) * (1 + inner // width) + inner // parts
    row = lambda w: pl.BlockSpec((tile, w), lambda i: (i, 0))
    tok = pl.BlockSpec((parts, tile, wide), lambda i: (0, i, 0))
    once = lambda a, b: pl.BlockSpec((a, b), lambda i: (0, 0), pipeline_mode=pl.Buffered(1))
    return pl.pallas_call(
        functools.partial(forward_back_kernel, 512),
        grid=(rows // tile,),
        in_specs=[
            pl.BlockSpec(memory_space=pltpu.SMEM),
            row(width),
            tok,
            row(width),
            once(width, width),
            once(width, inner),
            once(inner, width),
            once(4, width),
        ],
        out_specs=[
            row(width),
            row(width),
            tok,
            pl.BlockSpec((parts, packed, width), lambda i: (0, 0, 0)),
            pl.BlockSpec((4, width), lambda i: (0, 0)),
        ],
        out_shape=[
            shape((rows, width), HALF),
            shape((rows, width), SINGLE),
            shape((parts, rows, wide), HALF),
            shape((parts, packed, width), HALF),
            shape((4, width), SINGLE),
        ],
        scratch_shapes=[
            pltpu.VMEM((width, width), SINGLE),
            pltpu.VMEM((width, inner), SINGLE),
            pltpu.VMEM((width, inner), SINGLE),
            pltpu.VMEM((tile, inner), HALF),
            pltpu.VMEM((tile, inner), SINGLE),
        ],
        compiler_params=pltpu.CompilerParams(vmem_limit_bytes=VMEM_LIMIT),
        cost_estimate=pl.CostEstimate(
            flops=18 * 10**9, bytes_accessed=20 * 10**6, transcendentals=5 * 10**6
        ),
        name="forward_back",
    )(me, x, ctx, dy, wo, wh, wp, vec)


def attend_back_kernel(
    heads,
    order_ref,
    x_ref,
    q_ref,
    k_ref,
    v_ref,
    kt_ref,
    ot_ref,
    lse_ref,
    do_ref,
    g_ref,
    dw_ref,
    dk_s,
    dv_s,
    dw_s,
):
    trees = q_ref.shape[0] // heads
    wide = heads * HEAD

    def tree_step(tree, _):
        dk_s[...] = jnp.zeros_like(dk_s)
        dv_s[...] = jnp.zeros_like(dv_s)
        for start, keys in tile_list():
            here = slice(start, start + PAIR)
            rows = pair_rows(order_ref, tree, start)
            grad = jnp.concatenate([do_ref[r, :] for r in rows], axis=0)
            prod = grad.T.astype(SINGLE) * ot_ref[tree, :, here]
            grads = []
            for h in range(heads):
                at = tree * heads + h
                cols = slice(h * HEAD, (h + 1) * HEAD)
                q = q_ref[at, here, :]
                do = grad[:, cols]
                lse = lse_ref[at, :, here]
                delta = jnp.sum(prod[cols], axis=0, keepdims=True)
                dq = 0.0
                for off, size, kind in keys:
                    span = slice(off, off + size)
                    p = jnp.exp2(dot(k_ref[at, span, :], q, NT) * SCALE - lse)
                    if kind:
                        p = jnp.where(mask_of(kind), p, 0.0)
                    dp = dot(v_ref[at, span, :], do, NT)
                    ds = (p * (dp - delta)).astype(HALF)
                    dv_s[h, span, :] += dot(p.astype(HALF), do)
                    dk_s[h, span, :] += dot(ds, q)
                    dq = dq + dot(kt_ref[at, :, span], ds)
                grads.append(dq * 0.125)
            dq = (jnp.concatenate(grads, axis=0) if heads > 1 else grads[0]).T.astype(HALF)
            for i, r in enumerate(rows):
                g_ref[r, 0:wide] = dq[i * BLOCK : (i + 1) * BLOCK]
        for start in range(0, TREE_TOK, PAIR):
            here = slice(start, start + PAIR)
            dk = [dk_s[h, here, :] * 0.125 for h in range(heads)]
            dv = [dv_s[h, here, :] for h in range(heads)]
            both = jnp.concatenate(dk + dv, axis=-1).astype(HALF)
            for i, r in enumerate(pair_rows(order_ref, tree, start)):
                g_ref[r, wide : 3 * wide] = both[i * BLOCK : (i + 1) * BLOCK]
        return 0

    lax.fori_loop(0, trees, tree_step, 0)
    dw_s[...] = jnp.zeros_like(dw_s)
    step = 4 * BLOCK

    def weight_step(i, _):
        r = pl.ds(pl.multiple_of(i * step, step), step)
        dw_s[...] += dot(g_ref[r, :].T, x_ref[r, :])
        return 0

    lax.fori_loop(0, x_ref.shape[0] // step, weight_step, 0)
    dw_ref[...] = dw_s[...].astype(HALF)


def attend_back(order, x, saved, do, heads):
    total, width = x.shape
    wide = heads * HEAD
    return pl.pallas_call(
        functools.partial(attend_back_kernel, heads),
        out_shape=[shape((total, 3 * wide), HALF), shape((3 * wide, width), HALF)],
        in_specs=[pl.BlockSpec(memory_space=pltpu.SMEM)] + vmem(8),
        out_specs=vmem(2),
        scratch_shapes=[
            pltpu.VMEM((heads, TREE_TOK, HEAD), SINGLE),
            pltpu.VMEM((heads, TREE_TOK, HEAD), SINGLE),
            pltpu.VMEM((3 * wide, width), SINGLE),
        ],
        compiler_params=pltpu.CompilerParams(vmem_limit_bytes=VMEM_LIMIT),
        cost_estimate=pl.CostEstimate(
            flops=25 * 10**9, bytes_accessed=30 * 10**6, transcendentals=11 * 10**6
        ),
        name="attend_back",
    )(order, x, *saved, do)


def input_kernel(me_ref, base_ref, g_ref, w_ref, out_ref):
    me = me_ref[0]
    total = base_ref[...]
    for r in range(g_ref.shape[0]):
        total = total + dot(g_ref[r], w_ref[r ^ me], NT)
    out_ref[...] = total


def input_gradient(me, base, grads, weights):
    rows, width = base.shape
    parts, _, wide = grads.shape
    tile = PAIR if rows % PAIR == 0 else BLOCK
    row = pl.BlockSpec((tile, width), lambda i: (i, 0))
    return pl.pallas_call(
        input_kernel,
        grid=(rows // tile,),
        in_specs=[
            pl.BlockSpec(memory_space=pltpu.SMEM),
            row,
            pl.BlockSpec((parts, tile, wide), lambda i: (0, i, 0)),
            pl.BlockSpec(
                (parts, width, wide), lambda i: (0, 0, 0), pipeline_mode=pl.Buffered(1)
            ),
        ],
        out_specs=row,
        out_shape=shape((rows, width), SINGLE),
        compiler_params=pltpu.CompilerParams(vmem_limit_bytes=VMEM_LIMIT),
        cost_estimate=pl.CostEstimate(
            flops=2 * 10**9, bytes_accessed=11 * 10**6, transcendentals=0
        ),
        name="input_gradient",
    )(me, base, grads, weights)


def swap(value, axis, size, bit):
    return lax.ppermute(value, axis, [(i, i ^ bit) for i in range(size)])


def gather_near(value, parts):
    if parts != 4:
        return [value] + [swap(value, "fsdp", parts, r) for r in range(1, parts)]
    half = value.shape[0] // 2
    first = swap(value, "fsdp", parts, 1)
    second = swap(value, "fsdp", parts, 2)
    upper = swap(first[:half], "fsdp", parts, 2)
    lower = swap(second[half:], "fsdp", parts, 1)
    return [value, first, second, jnp.concatenate([upper, lower], axis=0)]


def exchange(value, parts):
    return jnp.stack([value[0]] + [swap(value[r], "fsdp", parts, r) for r in range(1, parts)])


def to_absolute(value, me):
    bit = 1
    while bit < value.shape[0]:
        flipped = value.reshape((-1, 2, bit) + value.shape[1:])[:, ::-1].reshape(value.shape)
        value = jnp.where((me & bit) != 0, flipped, value)
        bit *= 2
    return value


def shards(
    parts,
    inputs,
    cotangent,
    segments,
    trees,
    parents,
    w_query,
    w_key,
    w_value,
    w_out,
    w_hidden,
    w_proj,
    norm1_gain,
    norm1_bias,
    norm2_gain,
    norm2_bias,
):
    x = inputs[0]
    rows, width = x.shape
    inner = w_hidden.shape[1]
    heads = HEADS // parts
    wide = heads * HEAD
    depth = width // parts
    me = lax.axis_index("fsdp")
    me_arg = me.astype(jnp.int32).reshape(1)
    order = block_order(segments[0], trees[0], parents[0], rows, me)

    small = jnp.concatenate([w_query, w_key, w_value, w_out], axis=1)
    small_all = lax.all_gather(small, "fsdp", axis=0, tiled=True)
    near = jnp.concatenate(gather_near(x, parts), axis=0)
    full_h = lax.all_gather(w_hidden, "fsdp", axis=0, tiled=True)
    full_p = lax.all_gather(w_proj, "fsdp", axis=0, tiled=True)
    full_o = small_all[:, 3 * width :]
    by_device = small_all[:, : 3 * width].reshape(width, 3, parts, wide)
    by_device = by_device.transpose(2, 0, 1, 3).reshape(parts, width, 3 * wide)
    own = lax.dynamic_index_in_dim(by_device, me, 0, keepdims=False)

    ctx, *saved = attend(order, near, own, heads)
    ctx = exchange(ctx.reshape(parts, rows, wide), parts)
    vec = jnp.stack([norm1_gain, norm1_bias, norm2_gain, norm2_bias])
    output, dh1, dctx, pack, norms = forward_back(
        me_arg, x, ctx, cotangent[0], full_o, full_h, full_p, vec
    )
    do = exchange(dctx, parts).reshape(parts * rows, wide)
    grads, dw = attend_back(order, near, saved, do, heads)
    grads = exchange(grads.reshape(parts, rows, 3 * wide), parts)
    input_grad = input_gradient(me_arg, dh1, grads, by_device)

    pack = exchange(pack, parts).astype(SINGLE).sum(axis=0).astype(HALF)
    pack = lax.psum(pack, "rep").astype(SINGLE)
    grad_out = pack[:depth]
    base = depth * (1 + inner // width)
    grad_hidden = (
        pack[depth:base].reshape(inner // width, depth, width).transpose(1, 0, 2)
    ).reshape(depth, inner)
    cols = inner // parts
    grad_proj = pack[base:].reshape(cols, width // cols, cols).transpose(2, 1, 0)
    grad_proj = grad_proj.reshape(cols, width)

    dw = lax.psum(dw, "rep")
    dw = dw.reshape(3 * wide, parts, depth).transpose(1, 0, 2)
    dw = to_absolute(exchange(to_absolute(dw, me), parts), me).astype(SINGLE)
    dw = dw.reshape(parts, 3, wide, depth).transpose(1, 3, 0, 2).reshape(3, depth, width)
    norms = lax.psum(norms, ("fsdp", "rep"))
    return (
        output[None],
        input_grad[None],
        dw[0],
        dw[1],
        dw[2],
        grad_out,
        grad_hidden,
        grad_proj,
        norms[0],
        norms[1],
        norms[2],
        norms[3],
    )


def solution(mesh):
    token = P("rep", "fsdp", None)
    weight = P("fsdp", None)
    placed = (token, token, P("rep", None), P("rep", None), P("rep", None, None))
    return jax.shard_map(
        functools.partial(shards, mesh.shape["fsdp"]),
        mesh=mesh,
        in_specs=placed + (weight,) * 6 + (P(),) * 4,
        out_specs=(token, token) + (weight,) * 6 + (P(),) * 4,
        check_vma=False,
    )
```

time: 2080 us -> 422 us (0.20)
  matrix products: 920 us -> 0 us
  other arithmetic: 407 us -> 18.7 us
  local copies, waits for them, and re-layouts: 321 us -> 34.4 us
  waiting for transfers between devices: 297 us -> 122 us
  Pallas kernels: 0 us -> 138 us
  starting transfers between devices: 0.79 us -> 24.4 us
  blocking collectives: 88.7 us -> 66 us
    dot_general x198 -> x0, matrix products: 920 us -> none  [the longest x60 279 us: scores_of(): jnp.einsum('rhd,khd->hrk', q_heads, item[0], preferred_element_type=single)]
    and x240 -> x0, other arithmetic: 266 us -> none  [the longest x80 128 us: allowed_pair(): (tree_k[None, :] == tree_q[:, None]) & (same & (pos_k[None, :] <= pos_q[:...]
    reduce_scatter x5 -> x0, waiting for transfers between devices: 211 us -> none  [the longest x1 61 us: shards(): lax.psum_scatter(value_terms.astype(jnp.bfloat16), 'fsdp', scatter_dimens...]
    pallas_call x0 -> x4, Pallas kernels: none -> 138 us  [the longest x1 57.4 us: attend_back(): pl.pallas_call(functools.partial(attend_back_kernel, heads), out_shape=[s...]
    dynamic_slice x161 -> x2, local copies, waits for them, and re-layouts: 137 us -> 0.95 us  [shards(): own = lax.dynamic_index_in_dim(by_device, me, 0, keepdims=False)]
    reduce_sum x26 -> x4, other arithmetic: 128 us -> 4.16 us  [the longest x1 3.27 us: shards(): pack = exchange(pack, parts).astype(SINGLE).sum(axis=0).astype(HALF)]
    ppermute x0 -> x19, waiting for transfers between devices: none -> 108 us  [swap(): return lax.ppermute(value, axis, [(i, i ^ bit) for i in range(size)])]
    while x620 -> x0, local copies, waits for them, and re-layouts: 85.8 us -> none
  transfers between devices with their start and end apart: 13 -> 23, of which waited for: 10 -> 9; matrix products, arithmetic and copies ran while one was open for 38% -> 10% of each run, Pallas kernels for 0% -> 25%
where the time goes in v1:
time: 422 us; the launch traced here: 418 us
  Pallas kernels  138 us (33%)
  waiting for transfers between devices  122 us (29%)
  blocking collectives  66 us (16%)
  local copies, waits for them, and re-layouts  34.4 us (8%)
  starting transfers between devices  24.4 us (6%)
  other arithmetic  18.7 us (4%)
  between operations  14.3 us (3%)
    ppermute x19, waiting for transfers between devices, swap(): return lax.ppermute(value, axis, [(i, i ^ bit) for i in range(size)])  108 us
    psum x1, blocking collectives, shards(): norms = lax.psum(norms, ('fsdp', 'rep'))  66 us
    pallas_call x1, Pallas kernels, attend_back(): pl.pallas_call(functools.partial(attend_back_kernel, heads), out_shape=[s...  57.4 us
    pallas_call x1, Pallas kernels, attend(): pl.pallas_call(functools.partial(attend_kernel, heads), out_shape=[shape(...  38.6 us
    pallas_call x1, Pallas kernels, forward_back(): pl.pallas_call(functools.partial(forward_back_kernel, 512), grid=(rows //...  34 us
    ppermute x19, starting transfers between devices, swap(): return lax.ppermute(value, axis, [(i, i ^ bit) for i in range(size)])  24.3 us
    psum x1, waiting for transfers between devices, shards(): dw = lax.psum(dw, 'rep')  12.8 us
    unnamed x28, local copies, waits for them, and re-layouts  9.67 us
  transfers between devices with their start and end apart: 23, of which 9 were waited for; matrix products, arithmetic and copies ran while one was open for 10% of the time, Pallas kernels for 25%

profile of v1, /device:TPU:0, one launch (start us, length us, event | category | flops | bytes accessed | tf_op | source)
XLA Modules:
  0.0 417.6 jit_solution(10351719771378550847)
XLA Ops:
  7.3 1.9 pad_maximum_fusion.3
  10.0 3.0 collective-permute-start
  15.4 2.5 constant_dynamic-update-slice_fusion.4
  17.9 36.5 %collective-permute-done = bf16[1280,512]{1,0:T(8,128)(2,1)S(1)} collective-permute-done((bf16[1280,512]{1,0:T(8,128)(2,1)}, bf16[1280,512]{1,0:T(8,128)(2,1)S(1)}, u32[]{:S(2)}, u32[]{:S(2)}) %collective-permute-start) | collective-permute-done | bytes 1310752 | tf_op jit(solution)/shard_map/ppermute | solution.py:474
  56.4 2.2 collective-permute-done.1
  61.3 13.1 %collective-permute-done.2 = bf16[640,512]{1,0:T(8,128)(2,1)S(1)} collective-permute-done((bf16[640,512]{1,0:T(8,128)(2,1)S(1)}, bf16[640,512]{1,0:T(8,128)(2,1)S(1)}, u32[]{:S(2)}, u32[]{:S(2)}) %collective-permute-start.2) | collective-permute-done | bytes 655392 | tf_op jit(solution)/shard_map/ppermute | solution.py:474
  80.4 38.6 %attend.1 = (bf16[5120,128]{1,0:T(8,128)(2,1)}, bf16[4,2560,64]{2,1,0:T(8,128)(2,1)}, bf16[4,2560,64]{2,1,0:T(8,128)(2,1)}, bf16[4,2560,64]{2,1,0:T(8,128)(2,1)}...) custom-call(s32[40]{0:T(128)} %select_reduce_fusion.order_ref, ...), custom_call_target="tpu_custom_call" | custom-call | flops 10000000000 | bytes 20000000 | tf_op jit(solution)/shard_map/attend/pallas_call | solution.py:164
  128.1 15.1 %collective-permute-done.5 = bf16[1280,128]{1,0:T(8,128)(2,1)S(1)} collective-permute-done((bf16[1280,128]{1,0:T(8,128)(2,1)S(1)}, bf16[1280,128]{1,0:T(8,128)(2,1)S(1)}, u32[]{:S(2)}, u32[]{:S(2)}) %collective-permute-start.5) | collective-permute-done | bytes 327712 | tf_op jit(solution)/shard_map/ppermute | solution.py:474
  143.1 5.6 %collective-permute-done.4 = bf16[1280,128]{1,0:T(8,128)(2,1)} collective-permute-done((bf16[1280,128]{1,0:T(8,128)(2,1)S(1)}, bf16[1280,128]{1,0:T(8,128)(2,1)}, u32[]{:S(2)}, u32[]{:S(2)}) %collective-permute-start.4) | collective-permute-done | bytes 327712 | tf_op jit(solution)/shard_map/ppermute | solution.py:474
  148.7 2.2 pad_maximum_fusion.1.ctx_ref
  150.9 34.0 %forward_back.1 = (bf16[1280,512]{1,0:T(8,128)(2,1)}, f32[1280,512]{1,0:T(8,128)}, bf16[4,1280,128]{2,1,0:T(8,128)(2,1)}, bf16[4,1152,512]{2,1,0:T(8,128)(2,1)}, f32[4,512]{1,0:T(4,128)}) custom-call(s32[1]{0:T(128)} %bitcast.me_ref, bf16[1280,512]{1,0:T(8,128)(2,1)} %bitcast.1.x_ref, bf16[4,1280,128]{2,1,0:T(8,128)(2,1)} %pad_maximum_fusion.1.ctx_ref, ...), custom_call_target="tpu_custom_call" | custom-call | flops 17999998976 | bytes 20000000 | tf_op jit(solution)/shard_map/forward_back/pallas_call | solution.py:303
  184.9 2.2 fusion.13
  190.6 3.2 slice_bitcast_fusion.2
  195.8 66.0 %psum.23 = f32[4,512]{1,0:T(4,128)S(1)} all-reduce(f32[4,512]{1,0:T(4,128)S(1)} %copy-done.4), channel_id=1, replica_groups=mesh['fsdp'=4,'rep'=8] {'fsdp','rep'}, use_global_device_ids=true, to_apply=%region_5.6 | all-reduce | flops 2048 | bytes 16384 | tf_op jit(solution)/shard_map/psum | solution.py:565
  261.7 2.2 collective-permute-start.18
  263.9 2.3 pad_maximum_fusion.2
  266.2 57.4 %attend_back.1 = (bf16[5120,384]{1,0:T(8,128)(2,1)}, bf16[384,512]{1,0:T(8,128)(2,1)}) custom-call(s32[40]{0:T(128)} %select_reduce_fusion.order_ref, bf16[5120,512]{1,0:T(8,128)(2,1)} %constant_dynamic-update-slice_fusion.x_ref, bf16[4,2560,64]{2,1,0:T(8,128)(2,1)} %get-tuple-element.29.q_ref, bf16[4,2560,64]{2,1,0:T(8,128)(2,1)} %get-tuple-element.30.k_ref, ...), custom_call_target="tpu_custom_call" | custom-call | flops 24999999488 | bytes 30000000 | tf_op jit(solution)/shard_map/attend_back/pallas_call | solution.py:421
  323.6 3.8 slice_bitcast_fusion.4
  331.7 3.3 fusion.1
  335.6 16.8 %collective-permute-done.10 = bf16[1280,384]{1,0:T(8,128)(2,1)} collective-permute-done((bf16[1280,384]{1,0:T(8,128)(2,1)}, bf16[1280,384]{1,0:T(8,128)(2,1)}, u32[]{:S(2)}, u32[]{:S(2)}) %collective-permute-start.10) | collective-permute-done | bytes 983072 | tf_op jit(solution)/shard_map/ppermute | solution.py:474
  352.4 19.0 %collective-permute-done.11 = bf16[1280,384]{1,0:T(8,128)(2,1)} collective-permute-done((bf16[1280,384]{1,0:T(8,128)(2,1)}, bf16[1280,384]{1,0:T(8,128)(2,1)}, u32[]{:S(2)}, u32[]{:S(2)}) %collective-permute-start.11) | collective-permute-done | bytes 983072 | tf_op jit(solution)/shard_map/ppermute | solution.py:474
  371.4 3.6 pad_maximum_fusion.g_ref
  375.0 7.9 %input_gradient.1 = f32[1280,512]{1,0:T(8,128)} custom-call(s32[1]{0:T(128)} %bitcast.me_ref, f32[1280,512]{1,0:T(8,128)} %get-tuple-element.28.base_ref, bf16[4,1280,384]{2,1,0:T(8,128)(2,1)} %pad_maximum_fusion.g_ref, bf16[4,512,384]{2,1,0:T(8,128)(2,1)} %copy.60.w_ref), custom_call_target="tpu_custom_call" | custom-call | flops 2000000000 | bytes 11000000 | tf_op jit(solution)/shard_map/input_gradient/pallas_call | solution.py:452
  382.9 12.8 %all-reduce.3.cloned.1.call-done = (bf16[4,384,128]{2,1,0:T(8,128)(2,1)}, bf16[1152,512]{1,0:T(8,128)(2,1)}) async-done(((bf16[4,384,128]{2,1,0:T(8,128)(2,1)}, bf16[1152,512]{1,0:T(8,128)(2,1)}), (bf16[4,384,128]{2,1,0:T(8,128)(2,1)}, bf16[1152,512]{1,0:T(8,128)(2,1)})) %all-reduce.3.cloned.1.call-update) | async-done | bytes 1572880 | tf_op jit(solution)/shard_map/psum | solution.py:561
  (108 shorter events, 48.3 us)
Async XLA Ops:
  7.2 7.5 %copy-start.2 = (s32[1,5120]{1,0:T(1,128)S(1)}, s32[1,5120]{1,0:T(1,128)}, u32[]{:S(2)}) copy-start(s32[1,5120]{1,0:T(1,128)} %param.18) | copy-start | bytes 61444
  7.2 69.0 %all-gather.4.cloned.1.call-start = ((), (), s32[]{:S(2)}) async-start(), calls=%async_computation | async-start | bytes 2621440 | tf_op jit(solution)/shard_map/all_gather | solution.py:530
  9.2 141.7 %all-gather.6.cloned.1.call-start = ((), (), s32[]{:S(2)}) async-start(), calls=%async_computation.1 | async-start | bytes 2621440 | tf_op jit(solution)/shard_map/all_gather | solution.py:532
  10.0 140.9 %all-gather.8.cloned.1.call-start = ((), (), s32[]{:S(2)}) async-start(), calls=%async_computation.2 | async-start | bytes 2621440 | tf_op jit(solution)/shard_map/all_gather | solution.py:533
  10.0 44.4 %collective-permute-start = (bf16[1280,512]{1,0:T(8,128)(2,1)}, bf16[1280,512]{1,0:T(8,128)(2,1)S(1)}, u32[]{:S(2)}, u32[]{:S(2)}) collective-permute-start(bf16[1280,512]{1,0:T(8,128)(2,1)} %bitcast.1.x_ref), channel_id=1, source_target_pairs={{0,8},{8,0},{16,24},{24,16},{1,9},{9,1},{17,25},{25,17},{2,10},{10... | collective-permute-start | bytes 3932168 | tf_op jit(solution)/shard_map/ppermute | solution.py:474
  13.0 45.6 %collective-permute-start.1 = (bf16[1280,512]{1,0:T(8,128)(2,1)}, bf16[1280,512]{1,0:T(8,128)(2,1)S(1)}, u32[]{:S(2)}, u32[]{:S(2)}) collective-permute-start(bf16[1280,512]{1,0:T(8,128)(2,1)} %bitcast.1.x_ref), channel_id=1, source_target_pairs={{0,16},{8,24},{16,0},{24,8},{1,17},{9,25},{17,1},{25,9},{2,18},{10... | collective-permute-start | bytes 3932168 | tf_op jit(solution)/shard_map/ppermute | solution.py:474
  14.6 381.2 %all-reduce.3.cloned.1.call-start = ((), (), s32[]{:S(2)}) async-start(), calls=%async_computation.3 | async-start | bytes 3145728 | tf_op jit(solution)/shard_map/psum | solution.py:561
  54.4 19.9 %collective-permute-start.2 = (bf16[640,512]{1,0:T(8,128)(2,1)S(1)}, bf16[640,512]{1,0:T(8,128)(2,1)S(1)}, u32[]{:S(2)}, u32[]{:S(2)}) collective-permute-start(bf16[640,512]{1,0:T(8,128)(2,1)S(1)} %slice.163), channel_id=1, source_target_pairs={{0,16},{8,24},{16,0},{24,8},{1,17},{9,25},{17,1},{25,9},{2,18},{10... | collective-permute-start | bytes 1966088 | tf_op jit(solution)/shard_map/ppermute | solution.py:474
  58.7 16.6 %collective-permute-start.3 = (bf16[640,512]{1,0:T(8,128)(2,1)S(1)}, bf16[640,512]{1,0:T(8,128)(2,1)S(1)}, u32[]{:S(2)}, u32[]{:S(2)}) collective-permute-start(bf16[640,512]{1,0:T(8,128)(2,1)S(1)} %slice.164), channel_id=1, source_target_pairs={{0,8},{8,0},{16,24},{24,16},{1,9},{9,1},{17,25},{25,17},{2,10},{10... | collective-permute-start | bytes 1966088 | tf_op jit(solution)/shard_map/ppermute | solution.py:474
  120.4 22.7 %collective-permute-start.5 = (bf16[1280,128]{1,0:T(8,128)(2,1)S(1)}, bf16[1280,128]{1,0:T(8,128)(2,1)S(1)}, u32[]{:S(2)}, u32[]{:S(2)}) collective-permute-start(bf16[1280,128]{1,0:T(8,128)(2,1)S(1)} %get-tuple-element.106), channel_id=1, source_target_pairs={{0,16},{8,24},{16,0},{24,8},{1,17},{9,25},{17,1},{25,9},{2,18},{10... | collective-permute-start | bytes 983048 | tf_op jit(solution)/shard_map/ppermute | solution.py:474
  122.0 21.2 %collective-permute-start.6 = (bf16[1280,128]{1,0:T(8,128)(2,1)S(1)}, bf16[1280,128]{1,0:T(8,128)(2,1)S(1)}, u32[]{:S(2)}, u32[]{:S(2)}) collective-permute-start(bf16[1280,128]{1,0:T(8,128)(2,1)S(1)} %get-tuple-element.105), channel_id=1, source_target_pairs={{0,24},{8,16},{16,8},{24,0},{1,25},{9,17},{17,9},{25,1},{2,26},{10... | collective-permute-start | bytes 983048 | tf_op jit(solution)/shard_map/ppermute | solution.py:474
  122.3 26.4 %collective-permute-start.4 = (bf16[1280,128]{1,0:T(8,128)(2,1)S(1)}, bf16[1280,128]{1,0:T(8,128)(2,1)}, u32[]{:S(2)}, u32[]{:S(2)}) collective-permute-start(bf16[1280,128]{1,0:T(8,128)(2,1)S(1)} %get-tuple-element.107), channel_id=1, source_target_pairs={{0,8},{8,0},{16,24},{24,16},{1,9},{9,1},{17,25},{25,17},{2,10},{10... | collective-permute-start | bytes 983048 | tf_op jit(solution)/shard_map/ppermute | solution.py:474
  187.1 74.6 %collective-permute-start.7 = (bf16[1280,128]{1,0:T(8,128)(2,1)}, bf16[1280,128]{1,0:T(8,128)(2,1)S(1)}, u32[]{:S(2)}, u32[]{:S(2)}) collective-permute-start(bf16[1280,128]{1,0:T(8,128)(2,1)} %get-tuple-element.103), channel_id=1, source_target_pairs={{0,8},{8,0},{16,24},{24,16},{1,9},{9,1},{17,25},{25,17},{2,10},{10... | collective-permute-start | bytes 983048 | tf_op jit(solution)/shard_map/ppermute | solution.py:474
  187.4 76.5 %collective-permute-start.8 = (bf16[1280,128]{1,0:T(8,128)(2,1)}, bf16[1280,128]{1,0:T(8,128)(2,1)}, u32[]{:S(2)}, u32[]{:S(2)}) collective-permute-start(bf16[1280,128]{1,0:T(8,128)(2,1)} %get-tuple-element.102), channel_id=1, source_target_pairs={{0,16},{8,24},{16,0},{24,8},{1,17},{9,25},{17,1},{25,9},{2,18},{10... | collective-permute-start | bytes 983048 | tf_op jit(solution)/shard_map/ppermute | solution.py:474
  189.0 74.8 %collective-permute-start.9 = (bf16[1280,128]{1,0:T(8,128)(2,1)S(1)}, bf16[1280,128]{1,0:T(8,128)(2,1)}, u32[]{:S(2)}, u32[]{:S(2)}) collective-permute-start(bf16[1280,128]{1,0:T(8,128)(2,1)S(1)} %get-tuple-element.101), channel_id=1, source_target_pairs={{0,24},{8,16},{16,8},{24,0},{1,25},{9,17},{17,9},{25,1},{2,26},{10... | collective-permute-start | bytes 983048 | tf_op jit(solution)/shard_map/ppermute | solution.py:474
  193.8 135.2 %collective-permute-start.16 = (bf16[1152,512]{1,0:T(8,128)(2,1)}, bf16[1152,512]{1,0:T(8,128)(2,1)}, u32[]{:S(2)}, u32[]{:S(2)}) collective-permute-start(bf16[1152,512]{1,0:T(8,128)(2,1)} %get-tuple-element.93), channel_id=1, source_target_pairs={{0,8},{8,0},{16,24},{24,16},{1,9},{9,1},{17,25},{25,17},{2,10},{10... | collective-permute-start | bytes 3538952 | tf_op jit(solution)/shard_map/ppermute | solution.py:474
  194.1 137.6 %collective-permute-start.17 = (bf16[1152,512]{1,0:T(8,128)(2,1)S(1)}, bf16[1152,512]{1,0:T(8,128)(2,1)}, u32[]{:S(2)}, u32[]{:S(2)}) collective-permute-start(bf16[1152,512]{1,0:T(8,128)(2,1)S(1)} %get-tuple-element.95), channel_id=1, source_target_pairs={{0,16},{8,24},{16,0},{24,8},{1,17},{9,25},{17,1},{25,9},{2,18},{10... | collective-permute-start | bytes 3538952 | tf_op jit(solution)/shard_map/ppermute | solution.py:474
  261.7 70.0 %collective-permute-start.18 = (bf16[1152,512]{1,0:T(8,128)(2,1)S(1)}, bf16[1152,512]{1,0:T(8,128)(2,1)S(1)}, u32[]{:S(2)}, u32[]{:S(2)}) collective-permute-start(bf16[1152,512]{1,0:T(8,128)(2,1)S(1)} %get-tuple-element.94), channel_id=1, source_target_pairs={{0,24},{8,16},{16,8},{24,0},{1,25},{9,17},{17,9},{25,1},{2,26},{10... | collective-permute-start | bytes 3538952 | tf_op jit(solution)/shard_map/ppermute | solution.py:474
  327.4 25.0 %collective-permute-start.10 = (bf16[1280,384]{1,0:T(8,128)(2,1)}, bf16[1280,384]{1,0:T(8,128)(2,1)}, u32[]{:S(2)}, u32[]{:S(2)}) collective-permute-start(bf16[1280,384]{1,0:T(8,128)(2,1)} %get-tuple-element.99), channel_id=1, source_target_pairs={{0,8},{8,0},{16,24},{24,16},{1,9},{9,1},{17,25},{25,17},{2,10},{10... | collective-permute-start | bytes 2949128 | tf_op jit(solution)/shard_map/ppermute | solution.py:474
  329.0 42.4 %collective-permute-start.11 = (bf16[1280,384]{1,0:T(8,128)(2,1)}, bf16[1280,384]{1,0:T(8,128)(2,1)}, u32[]{:S(2)}, u32[]{:S(2)}) collective-permute-start(bf16[1280,384]{1,0:T(8,128)(2,1)} %get-tuple-element.98), channel_id=1, source_target_pairs={{0,16},{8,24},{16,0},{24,8},{1,17},{9,25},{17,1},{25,9},{2,18},{10... | collective-permute-start | bytes 2949128 | tf_op jit(solution)/shard_map/ppermute | solution.py:474
  329.1 42.4 %collective-permute-start.12 = (bf16[1280,384]{1,0:T(8,128)(2,1)}, bf16[1280,384]{1,0:T(8,128)(2,1)}, u32[]{:S(2)}, u32[]{:S(2)}) collective-permute-start(bf16[1280,384]{1,0:T(8,128)(2,1)} %get-tuple-element.97), channel_id=1, source_target_pairs={{0,24},{8,16},{16,8},{24,0},{1,25},{9,17},{17,9},{25,1},{2,26},{10... | collective-permute-start | bytes 2949128 | tf_op jit(solution)/shard_map/ppermute | solution.py:474
  398.7 7.1 %collective-permute-start.13 = (bf16[384,128]{1,0:T(8,128)(2,1)}, bf16[384,128]{1,0:T(8,128)(2,1)S(1)}, u32[]{:S(2)}, u32[]{:S(2)}) collective-permute-start(bf16[384,128]{1,0:T(8,128)(2,1)} %get-tuple-element.114), channel_id=1, source_target_pairs={{0,8},{8,0},{16,24},{24,16},{1,9},{9,1},{17,25},{25,17},{2,10},{10... | collective-permute-start | bytes 294920 | tf_op jit(solution)/shard_map/ppermute | solution.py:474
  398.8 7.0 %collective-permute-start.14 = (bf16[384,128]{1,0:T(8,128)(2,1)}, bf16[384,128]{1,0:T(8,128)(2,1)}, u32[]{:S(2)}, u32[]{:S(2)}) collective-permute-start(bf16[384,128]{1,0:T(8,128)(2,1)} %get-tuple-element.113), channel_id=1, source_target_pairs={{0,16},{8,24},{16,0},{24,8},{1,17},{9,25},{17,1},{25,9},{2,18},{10... | collective-permute-start | bytes 294920 | tf_op jit(solution)/shard_map/ppermute | solution.py:474
  400.2 5.8 %collective-permute-start.15 = (bf16[384,128]{1,0:T(8,128)(2,1)}, bf16[384,128]{1,0:T(8,128)(2,1)}, u32[]{:S(2)}, u32[]{:S(2)}) collective-permute-start(bf16[384,128]{1,0:T(8,128)(2,1)} %get-tuple-element.112), channel_id=1, source_target_pairs={{0,24},{8,16},{16,8},{24,0},{1,25},{9,17},{17,9},{25,1},{2,26},{10... | collective-permute-start | bytes 294920 | tf_op jit(solution)/shard_map/ppermute | solution.py:474
  (10 other events, 53.1 us)
Sparse Core Ops, SparseCore 0:
  10.5 54.6 all-gather.3
  67.0 34.7 all-gather.5
  103.7 44.8 all-gather.7
  335.1 60.5 all-reduce.2
